TPU v7x, 32 devices: a whole 2x2x4 slice. The times are simulated.
32 devices in a mesh: dp: 4 (over y, core), row: 2 (over x), col: 4 (over z).
Axes of the slice: x: 2, y: 2, z: 4, core: 2. Of those that a mesh axis runs over, the one named last changes fastest.
Arguments:
- inputs: bfloat16 [4096, 2048], P(('dp', 'col'), 'row'), may hold values from -6 to 6
- first_gain: float32 [1, 2048], P(None, 'row'), may hold values from 0.25 to 1.75
- first_shift: float32 [1, 2048], P(None, 'row'), may hold values from -3 to 3
- project_in: bfloat16 [1, 2048, 3, 2048], P(None, 'row', None, 'col'), may hold values from -0.125 to 0.125
- project_bias: float32 [1, 3, 2048], P(None, None, 'col'), may hold values from -3 to 3
- project_out: bfloat16 [1, 2048, 2048], P(None, 'col', 'row'), may hold values from -0.75 to 0.75
- second_gain: float32 [1, 2048], P(None, 'row'), may hold values from 0.25 to 1.75
- second_shift: float32 [1, 2048], P(None, 'row'), may hold values from -3 to 3
- gate_weight: bfloat16 [1, 2048, 2, 5632], P(None, 'row', None, 'col'), may hold values from -0.125 to 0.125
- down_weight: bfloat16 [1, 5632, 2048], P(None, 'col', 'row'), may hold values from -0.078125 to 0.078125
- cotangent: bfloat16 [4096, 2048], P(('dp', 'col'), 'row'), may hold values from -6 to 6
Outputs:
- layer_outputs: bfloat16 [1, 4096, 2048], P(None, ('dp', 'col'), 'row')
- input_grad: float32 [4096, 2048], P(('dp', 'col'), 'row')
- first_gain_grad: float32 [1, 2048], P(None, 'row')
- first_shift_grad: float32 [1, 2048], P(None, 'row')
- project_in_grad: float32 [1, 2048, 3, 2048], P(None, 'row', None, 'col')
- project_bias_grad: float32 [1, 3, 2048], P(None, None, 'col')
- project_out_grad: float32 [1, 2048, 2048], P(None, 'col', 'row')
- second_gain_grad: float32 [1, 2048], P(None, 'row')
- second_shift_grad: float32 [1, 2048], P(None, 'row')
- gate_weight_grad: float32 [1, 2048, 2, 5632], P(None, 'row', None, 'col')
- down_weight_grad: float32 [1, 5632, 2048], P(None, 'col', 'row')
All inputs are finite; a program needn't handle non-finite values.
Results may differ from a plain program's by a relative error of at most 0.015.
Values may be sent and summed in bfloat16 or wider, within the bound.
No kernel may reach another device: no remote copies, remote signals or barrier semaphores. Data moves between devices by JAX's collectives and lax.ppermute only.
A program may use at most 192 MiB of HBM per device.

v0:
```python
import math
import jax
import jax.numpy as jnp
from jax import lax
from jax.sharding import PartitionSpec as P

HEAD_DIM = 64
ROT = 16
LENGTH = 1024
EPSILON = 1e-05


def rotary_tables(tokens):
    position = (jnp.arange(tokens) % LENGTH).astype(jnp.float32)
    frequency = 10000.0 ** (-(jnp.arange(ROT // 2).astype(jnp.float32) * 2.0 / ROT))
    angles = position[:, None] * frequency[None, :]
    return (jnp.cos(angles), jnp.sin(angles))


def rotate(tensor, cosine_table, sine_table):
    half_rot = ROT // 2
    front_half = tensor[..., :half_rot]
    back_half = tensor[..., half_rot:ROT]
    cosine = cosine_table[:, None, :]
    sine = sine_table[:, None, :]
    return jnp.concatenate(
        [
            front_half * cosine - back_half * sine,
            back_half * cosine + front_half * sine,
            tensor[..., ROT:],
        ],
        axis=-1,
    )


def row_totals(first_part, second_part):
    return lax.psum((first_part, second_part), "row")


def norm_forward(stream, gain_row, shift_row):
    features = stream.shape[1] * lax.axis_size("row")
    summed, squares = row_totals(jnp.sum(stream, axis=1), jnp.sum(stream * stream, axis=1))
    average = summed / features
    variance = squares / features - average * average
    inv_root = lax.rsqrt(variance + EPSILON)
    normed = (stream - average[:, None]) * inv_root[:, None]
    return (normed, inv_root, (normed * gain_row + shift_row).astype(jnp.bfloat16))


def norm_backward(gradient, normed, inv_root, gain_row):
    features = gradient.shape[1] * lax.axis_size("row")
    scaled = gradient * gain_row
    summed, crossed = row_totals(jnp.sum(scaled, axis=1), jnp.sum(scaled * normed, axis=1))
    stream_grad = inv_root[:, None] * (
        scaled - summed[:, None] / features - normed * crossed[:, None] / features
    )
    return (stream_grad, jnp.sum(gradient * normed, axis=0), jnp.sum(gradient, axis=0))


def gather_tokens(local_low):
    return lax.all_gather(local_low, "col", axis=0, tiled=True)


def gather_gradient(local_low):
    return lax.all_gather(local_low, "col", axis=0, tiled=True)


def split_units(partial_sum):
    return lax.psum_scatter(partial_sum, "row", scatter_dimension=2, tiled=True)


def join_units(local_units):
    return lax.all_gather(local_units, "row", axis=1, tiled=True)


def split_unit_grads(partial_sum):
    return lax.psum_scatter(partial_sum, "row", scatter_dimension=1, tiled=True)


def join_unit_grads(local_units):
    return lax.all_gather(local_units, "row", axis=2, tiled=True)


def branch_sum(full_rows, weight_block):
    return lax.psum_scatter(
        jnp.dot(full_rows, weight_block, preferred_element_type=jnp.float32),
        "col",
        scatter_dimension=0,
        tiled=True,
    )


def input_sum(grad_full, weight_block):
    return lax.psum_scatter(
        jnp.einsum("stk,dtk->sd", grad_full, weight_block, preferred_element_type=jnp.float32),
        "col",
        scatter_dimension=0,
        tiled=True,
    )


def weight_product(normed, gain_row, shift_row, grad_full):
    local_low = (normed * gain_row + shift_row).astype(jnp.bfloat16)
    return jnp.einsum(
        "sd,stk->dtk",
        lax.all_gather(local_low, "col", axis=0, tiled=True),
        grad_full,
        preferred_element_type=jnp.float32,
    )


def block_scores(query_heads, key_heads, value_heads, block_index, factor):
    block_rows = min(512, LENGTH)
    offset = block_index * block_rows
    seq_begin = offset // LENGTH * LENGTH
    query_block = lax.dynamic_slice_in_dim(query_heads, offset, block_rows, 0)
    scores = (
        jnp.einsum("qhd,khd->hqk", query_block, key_heads, preferred_element_type=jnp.float32)
        * factor
    )
    query_position = offset - seq_begin + jnp.arange(block_rows)
    causal = query_position[:, None] >= jnp.arange(LENGTH)[None, :]
    scores = jnp.where(causal[None], scores, -jnp.inf)
    return (scores, query_block, key_heads, value_heads, offset, seq_begin)


def attend_forward(query_heads, key_heads, value_heads, factor):
    tokens = query_heads.shape[0]
    block_rows = min(512, LENGTH)

    def one_block(block_index):
        scores, query_block, key_block, value_block, offset, seq_begin = block_scores(
            query_heads, key_heads, value_heads, block_index, factor
        )
        highest = jnp.max(scores, axis=-1, keepdims=True)
        exponent = jnp.exp(scores - highest)
        summed = jnp.sum(exponent, axis=-1, keepdims=True)
        softmax_low = (exponent / summed).astype(jnp.bfloat16)
        attended = jnp.einsum(
            "hqk,khd->qhd", softmax_low, value_block, preferred_element_type=jnp.float32
        )
        return (attended, (highest + jnp.log(summed))[..., 0])

    attended, log_total = lax.map(one_block, jnp.arange(tokens // block_rows))
    return (attended.reshape(tokens, -1), log_total)


def attend_backward(query_heads, key_heads, value_heads, out_heads, log_total, factor):
    tokens = query_heads.shape[0]
    block_rows = min(512, LENGTH)

    def one_block(carry, block_index):
        key_grad, value_grad = carry
        scores, query_block, key_block, value_block, offset, seq_begin = block_scores(
            query_heads, key_heads, value_heads, block_index, factor
        )
        softmax_probs = jnp.exp(scores - log_total[block_index][..., None])
        grad_block = lax.dynamic_slice_in_dim(out_heads, offset, block_rows, 0)
        prob_grad = jnp.einsum(
            "qhd,khd->hqk", grad_block, value_block, preferred_element_type=jnp.float32
        )
        shift_term = jnp.sum(softmax_probs * prob_grad, axis=-1, keepdims=True)
        score_grad = (softmax_probs * (prob_grad - shift_term)).astype(jnp.bfloat16)
        query_grad = (
            jnp.einsum("hqk,khd->qhd", score_grad, key_block, preferred_element_type=jnp.float32)
            * factor
        )
        key_part = (
            jnp.einsum("hqk,qhd->khd", score_grad, query_block, preferred_element_type=jnp.float32)
            * factor
        )
        value_part = jnp.einsum(
            "hqk,qhd->khd",
            softmax_probs.astype(jnp.bfloat16),
            grad_block,
            preferred_element_type=jnp.float32,
        )
        key_grad = key_grad + key_part
        value_grad = value_grad + value_part
        return ((key_grad, value_grad), query_grad)

    zeros_start = jnp.zeros(key_heads.shape, jnp.float32)
    (key_grad, value_grad), query_grad = lax.scan(
        one_block, (zeros_start, zeros_start), jnp.arange(tokens // block_rows)
    )
    return (query_grad.reshape(key_heads.shape), key_grad, value_grad)


def local(
    inputs,
    first_gain,
    first_shift,
    project_in,
    project_bias,
    project_out,
    second_gain,
    second_shift,
    gate_weight,
    down_weight,
    cotangent,
):
    layers = project_in.shape[0]
    tokens = inputs.shape[0] * lax.axis_size("col")
    heads_here = project_in.shape[3] // lax.axis_size("row") // HEAD_DIM
    bias_width = project_bias.shape[2] // lax.axis_size("row")
    row_place = lax.axis_index("row")
    factor = 1.0 / math.sqrt(HEAD_DIM)
    cosine_table, sine_table = rotary_tables(tokens)
    stream = inputs.astype(jnp.float32)
    layer_index = 0
    normed_a, inv_root_a, low_a = norm_forward(
        stream, first_gain[layer_index], first_shift[layer_index]
    )
    full_a = gather_tokens(low_a)
    partial_mix = jnp.einsum(
        "sd,dtk->stk", full_a, project_in[layer_index], preferred_element_type=jnp.float32
    )
    bias_here = lax.dynamic_slice_in_dim(
        project_bias[layer_index], row_place * bias_width, bias_width, 1
    )
    mixed = (split_units(partial_mix) + bias_here[None]).reshape(tokens, 3, heads_here, HEAD_DIM)
    query_heads = rotate(mixed[:, 0], cosine_table, sine_table).astype(jnp.bfloat16)
    key_heads = rotate(mixed[:, 1], cosine_table, sine_table).astype(jnp.bfloat16)
    value_heads = mixed[:, 2].astype(jnp.bfloat16)
    attended, log_total = attend_forward(query_heads, key_heads, value_heads, factor)
    heads_full = join_units(attended.astype(jnp.bfloat16))
    residual = stream + branch_sum(heads_full, project_out[layer_index])
    normed_b, inv_root_b, low_b = norm_forward(
        residual, second_gain[layer_index], second_shift[layer_index]
    )
    full_b = gather_tokens(low_b)
    gate_up = split_units(
        jnp.einsum(
            "sd,dtf->stf", full_b, gate_weight[layer_index], preferred_element_type=jnp.float32
        )
    )
    hidden = (jax.nn.silu(gate_up[:, 0]) * gate_up[:, 1]).astype(jnp.bfloat16)
    hidden_full = join_units(hidden)
    layer_out = (residual + branch_sum(hidden_full, down_weight[layer_index])).astype(jnp.bfloat16)
    outputs = [layer_out]
    kept_a = None
    kept_b = None
    saved = [
        (
            normed_a,
            inv_root_a,
            kept_a,
            query_heads,
            key_heads,
            value_heads,
            log_total,
            heads_full,
            normed_b,
            inv_root_b,
            kept_b,
            gate_up,
            hidden_full,
        )
    ]
    gradient = cotangent.astype(jnp.float32)
    in_grads = [None] * layers
    bias_grads = [None] * layers
    out_grads = [None] * layers
    gate_grads = [None] * layers
    down_grads = [None] * layers
    gain_a_grads = [None] * layers
    shift_a_grads = [None] * layers
    gain_b_grads = [None] * layers
    shift_b_grads = [None] * layers
    for layer_index in reversed(range(layers)):
        (
            normed_a,
            inv_root_a,
            kept_a,
            query_heads,
            key_heads,
            value_heads,
            log_total,
            heads_full,
            normed_b,
            inv_root_b,
            kept_b,
            gate_up,
            hidden_full,
        ) = saved[layer_index]
        grad_full = gather_gradient(gradient.astype(jnp.bfloat16))
        down_grad = jnp.einsum(
            "sf,sd->fd", hidden_full, grad_full, preferred_element_type=jnp.float32
        )
        hidden_grad = split_unit_grads(
            jnp.einsum(
                "sd,fd->sf", grad_full, down_weight[layer_index], preferred_element_type=jnp.float32
            )
        )
        gate_value = gate_up[:, 0]
        up_value = gate_up[:, 1]
        sigmoid_gate = jax.nn.sigmoid(gate_value)
        gate_grad = (
            hidden_grad * up_value * sigmoid_gate * (1.0 + gate_value * (1.0 - sigmoid_gate))
        )
        up_grad = hidden_grad * gate_value * sigmoid_gate
        gate_up_grad = jnp.stack([gate_grad, up_grad], axis=1).astype(jnp.bfloat16)
        gate_up_full = join_unit_grads(gate_up_grad)
        gate_weight_grad = weight_product(
            normed_b, second_gain[layer_index], second_shift[layer_index], gate_up_full
        )
        normed_b_grad = input_sum(gate_up_full, gate_weight[layer_index])
        back_b, gain_b_grad, shift_b_grad = norm_backward(
            normed_b_grad, normed_b, inv_root_b, second_gain[layer_index]
        )
        gradient_two = gradient + back_b
        grad_two_full = gather_gradient(gradient_two.astype(jnp.bfloat16))
        out_grad_weight = jnp.einsum(
            "sk,sd->kd", heads_full, grad_two_full, preferred_element_type=jnp.float32
        )
        attended_grad = split_unit_grads(
            jnp.einsum(
                "sd,kd->sk",
                grad_two_full,
                project_out[layer_index],
                preferred_element_type=jnp.float32,
            )
        )
        attended_grad = attended_grad.astype(jnp.bfloat16).reshape(tokens, heads_here, HEAD_DIM)
        query_grad, key_grad, value_grad = attend_backward(
            query_heads, key_heads, value_heads, attended_grad, log_total, factor
        )
        query_grad = rotate(query_grad, cosine_table, -sine_table)
        key_grad = rotate(key_grad, cosine_table, -sine_table)
        mixed_grad = (
            jnp.stack([query_grad, key_grad, value_grad], axis=1)
            .reshape(tokens, 3, heads_here * HEAD_DIM)
            .astype(jnp.bfloat16)
        )
        mixed_full = join_unit_grads(mixed_grad)
        bias_grad = jnp.sum(mixed_full, axis=0, dtype=jnp.float32)
        in_grad = weight_product(
            normed_a, first_gain[layer_index], first_shift[layer_index], mixed_full
        )
        normed_a_grad = input_sum(mixed_full, project_in[layer_index])
        back_a, gain_a_grad, shift_a_grad = norm_backward(
            normed_a_grad, normed_a, inv_root_a, first_gain[layer_index]
        )
        gradient = gradient_two + back_a
        in_grads[layer_index] = in_grad
        bias_grads[layer_index] = bias_grad
        out_grads[layer_index] = out_grad_weight
        gate_grads[layer_index] = gate_weight_grad
        down_grads[layer_index] = down_grad
        gain_a_grads[layer_index] = gain_a_grad
        shift_a_grads[layer_index] = shift_a_grad
        gain_b_grads[layer_index] = gain_b_grad
        shift_b_grads[layer_index] = shift_b_grad
    stack_in = jnp.stack(in_grads)
    stack_bias = jnp.stack(bias_grads)
    stack_out = jnp.stack(out_grads)
    stack_gate = jnp.stack(gate_grads)
    stack_down = jnp.stack(down_grads)
    stack_in, stack_bias, stack_out, stack_gate, stack_down = (
        lax.psum(stack_in.astype(jnp.bfloat16), "dp").astype(jnp.float32),
        lax.psum(stack_bias.astype(jnp.bfloat16), "dp").astype(jnp.float32),
        lax.psum(stack_out.astype(jnp.bfloat16), "dp").astype(jnp.float32),
        lax.psum(stack_gate.astype(jnp.bfloat16), "dp").astype(jnp.float32),
        lax.psum(stack_down.astype(jnp.bfloat16), "dp").astype(jnp.float32),
    )
    gain_a_total, shift_a_total, gain_b_total, shift_b_total = lax.psum(
        (
            jnp.stack(gain_a_grads),
            jnp.stack(shift_a_grads),
            jnp.stack(gain_b_grads),
            jnp.stack(shift_b_grads),
        ),
        ("dp", "col"),
    )
    return (
        jnp.stack(outputs),
        gradient,
        gain_a_total,
        shift_a_total,
        stack_in,
        stack_bias,
        stack_out,
        gain_b_total,
        shift_b_total,
        stack_gate,
        stack_down,
    )


def solution(mesh):
    return jax.shard_map(
        local,
        mesh=mesh,
        in_specs=(
            P(("dp", "col"), "row"),
            P(None, "row"),
            P(None, "row"),
            P(None, "row", None, "col"),
            P(None, None, "col"),
            P(None, "col", "row"),
            P(None, "row"),
            P(None, "row"),
            P(None, "row", None, "col"),
            P(None, "col", "row"),
            P(("dp", "col"), "row"),
        ),
        out_specs=(
            P(None, ("dp", "col"), "row"),
            P(("dp", "col"), "row"),
            P(None, "row"),
            P(None, "row"),
            P(None, "row", None, "col"),
            P(None, None, "col"),
            P(None, "col", "row"),
            P(None, "row"),
            P(None, "row"),
            P(None, "row", None, "col"),
            P(None, "col", "row"),
        ),
        check_vma=False,
    )
```

profile of v0, /device:TPU:0, one launch (start us, length us, event | category | flops | bytes accessed | tf_op | source)
XLA Modules:
  0.0 1484.0 jit_solution(7739865274060016093)
XLA Ops:
  8.7 5.8 all-reduce.4
  17.3 47.9 %all-gather.9.cloned.1.call-done = bf16[1024,1024]{1,0:T(8,128)(2,1)} async-done(((bf16[256,1024]{1,0:T(8,128)(2,1)}), bf16[1024,1024]{1,0:T(8,128)(2,1)}) %all-gather.9.cloned.1.call-update) | async-done | bytes 2097168 | tf_op jit(solution)/shard_map/all_gather | solution.py:61
  65.1 6.9 fusion.42
  73.6 74.4 %reduce-scatter.9.cloned.1.call-done = f32[1024,3,256]{2,0,1:T(8,128)} async-done(((f32[1024,3,512]{2,0,1:T(8,128)}), f32[1024,3,256]{2,0,1:T(8,128)}) %reduce-scatter.9.cloned.1.call-update) | async-done | bytes 3145744 | tf_op jit(solution)/shard_map/reduce_scatter | solution.py:69
  148.0 3.8 broadcast_add_fusion
  151.8 3.5 copy.34
  160.4 21.1 %while.31 = (s32[]{:T(128)}, bf16[2,512,4,64]{1,3,2,0:T(8,128)(2,1)}, f32[2,4,512]{2,1,0:T(4,128)S(1)}, s32[2]{0:T(128)S(1)}, bf16[1024,4,64]{0,2,1:T(8,128)(2,1...) while((s32[]{:T(128)}, ...), condition=%wide.region_8.9_spmd, body=%wide.region_5.8_spmd.sunk | while | flops 562559488 | bytes 35459536 | solution.py:144
  184.1 21.4 %all-gather.11.cloned.1.call-done = bf16[1024,512]{0,1:T(8,128)(2,1)} async-done(((bf16[1024,256]{0,1:T(8,128)(2,1)}), bf16[1024,512]{0,1:T(8,128)(2,1)}) %all-gather.11.cloned.1.call-update) | async-done | bytes 1048592 | tf_op jit(solution)/shard_map/all_gather | solution.py:73
  205.5 4.8 fusion.77
  211.0 76.3 %reduce-scatter.11.cloned.1.call-done = f32[256,1024]{1,0:T(8,128)} async-done(((f32[1024,1024]{1,0:T(8,128)}), f32[256,1024]{1,0:T(8,128)}) %reduce-scatter.11.cloned.1.call-update) | async-done | bytes 1048592 | tf_op jit(solution)/shard_map/reduce_scatter | solution.py:85
  289.7 4.9 all-reduce.3
  297.3 37.9 %all-gather.17.cloned.1.call-done = bf16[1024,1024]{1,0:T(8,128)(2,1)} async-done(((bf16[256,1024]{1,0:T(8,128)(2,1)}), bf16[1024,1024]{1,0:T(8,128)(2,1)}) %all-gather.17.cloned.1.call-update) | async-done | bytes 2097168 | tf_op jit(solution)/shard_map/all_gather | solution.py:65
  335.2 8.2 fusion.44
  343.5 38.4 %all-gather.13.cloned.1.call-done = bf16[1024,1024]{1,0:T(8,128)(2,1)} async-done(((bf16[256,1024]{1,0:T(8,128)(2,1)}), bf16[1024,1024]{1,0:T(8,128)(2,1)}) %all-gather.13.cloned.1.call-update) | async-done | bytes 2097168 | tf_op jit(solution)/shard_map/all_gather | solution.py:61
  381.9 11.9 fusion.35
  393.9 61.0 %reduce-scatter.17.cloned.1.call-done = f32[1024,704]{0,1:T(8,128)} async-done(((f32[1024,1408]{0,1:T(8,128)}), f32[1024,704]{0,1:T(8,128)}) %reduce-scatter.17.cloned.1.call-update) | async-done | bytes 2883600 | tf_op jit(solution)/shard_map/reduce_scatter | solution.py:77
  454.9 136.2 %reduce-scatter.13.cloned.1.call-done = f32[1024,2,704]{0,2,1:T(8,128)} async-done(((f32[1024,2,1408]{0,2,1:T(8,128)}), f32[1024,2,704]{0,2,1:T(8,128)}) %reduce-scatter.13.cloned.1.call-update) | async-done | bytes 5767184 | tf_op jit(solution)/shard_map/reduce_scatter | solution.py:69
  591.1 5.3 fusion.59
  598.9 74.0 %all-gather.19.cloned.1.call-done = bf16[1024,2,1408]{0,2,1:T(8,128)(2,1)} async-done(((bf16[1024,2,704]{0,2,1:T(8,128)(2,1)}), bf16[1024,2,1408]{0,2,1:T(8,128)(2,1)}) %all-gather.19.cloned.1.call-update) | async-done | bytes 5767184 | tf_op jit(solution)/shard_map/all_gather | solution.py:81
  672.9 11.5 fusion.51
  684.4 32.5 %all-gather.15.cloned.1.call-done = bf16[1024,1408]{0,1:T(8,128)(2,1)} async-done(((bf16[1024,704]{0,1:T(8,128)(2,1)}), bf16[1024,1408]{0,1:T(8,128)(2,1)}) %all-gather.15.cloned.1.call-update) | async-done | bytes 2883600 | tf_op jit(solution)/shard_map/all_gather | solution.py:73
  716.9 8.2 fusion.46
  725.2 71.5 %reduce-scatter.19.cloned.1.call-done = f32[256,1024]{1,0:T(8,128)} async-done(((f32[1024,1024]{1,0:T(8,128)}), f32[256,1024]{1,0:T(8,128)}) %reduce-scatter.19.cloned.1.call-update) | async-done | bytes 1048592 | tf_op jit(solution)/shard_map/reduce_scatter | solution.py:94
  799.3 4.9 all-reduce.2
  804.2 72.5 %reduce-scatter.15.cloned.1.call-done = f32[256,1024]{1,0:T(8,128)} async-done(((f32[1024,1024]{1,0:T(8,128)}), f32[256,1024]{1,0:T(8,128)}) %reduce-scatter.15.cloned.1.call-update) | async-done | bytes 1048592 | tf_op jit(solution)/shard_map/reduce_scatter | solution.py:85
  876.7 3.8 fusion.87
  880.6 46.6 %all-gather.21.cloned.1.call-done = bf16[1024,1024]{1,0:T(8,128)(2,1)} async-done(((bf16[256,1024]{1,0:T(8,128)(2,1)}), bf16[1024,1024]{1,0:T(8,128)(2,1)}) %all-gather.21.cloned.1.call-update) | async-done | bytes 2097168 | tf_op jit(solution)/shard_map/all_gather | solution.py:65
  927.2 4.5 fusion.75
  931.7 8.6 all-gather.23.cloned.1.call-start
  940.3 22.0 %reduce-scatter.21.cloned.1.call-done = f32[1024,256]{1,0:T(8,128)} async-done(((f32[1024,512]{1,0:T(8,128)}), f32[1024,256]{1,0:T(8,128)}) %reduce-scatter.21.cloned.1.call-update) | async-done | bytes 1048592 | tf_op jit(solution)/shard_map/reduce_scatter | solution.py:77
  966.5 61.6 %while.32 = (s32[]{:T(128)}, f32[1024,4,64]{0,2,1:T(8,128)}, f32[1024,4,64]{0,2,1:T(8,128)}, f32[2,512,4,64]{1,0,3,2:T(2,128)}, s32[2]{0:T(128)S(1)}, /*index=5*...) while((s32[]{:T(128)}, f32[1024,4,64]{0,2,1:T(8,128)}, ...), condition=%wide.region_25.26_spmd.clone, body=%wide.region_23.25_spmd.clone.sunk | while | flops 1375599104 | bytes 91288184 | solution.py:183
  972.6 3.5 fusion.141
  986.3 10.4 dynamic_update_slice.28
  1002.8 4.5 fusion.141
  1017.6 10.4 dynamic_update_slice.28
  1049.1 7.3 fusion.39
  1056.4 11.2 convert_bitcast_fusion
  1069.9 24.0 %all-gather.23.cloned.1.call-done = bf16[1024,3,512]{2,0,1:T(8,128)(2,1)} async-done(((bf16[1024,3,256]{2,0,1:T(8,128)(2,1)}), bf16[1024,3,512]{2,0,1:T(8,128)(2,1)}) %all-gather.23.cloned.1.call-update) | async-done | bytes 3145744 | tf_op jit(solution)/shard_map/all_gather | solution.py:81
  1093.9 7.7 convert_bitcast_fusion.1
  1101.6 6.9 fusion.48
  1111.0 7.9 psum.130
  1119.4 208.6 %all-reduce.8.cloned.1.call-done = (bf16[1,1024,2,1408]{3,1,2,0:T(8,128)(2,1)}, bf16[1,1024,3,512]{3,1,2,0:T(8,128)(2,1)}, bf16[1,512,1024]{2,1,0:T(8,128)(2,1)}, bf16[1,1408,1024]{2,1,0:T(8,128)(2,1)}) async-done(((bf16[1,1024,2,1408]{3,1,2,0:T(8,128)(2,1)}, bf16[1,1024,3,512]{3,1,2,0:T(8,128)(2,1)}, bf16[1,512,1024]{2,1,0:T(8,128)(2,1)}, bf16[1,1408,1024]{2,1,0:T(8,128)(2,1)}), ...) | async-done | bytes 12845072 | tf_op jit(solution)/shard_map/psum | solution.py:363
  1330.8 12.8 copy.45
  1343.6 3.3 convert_element_type.211
  1346.9 3.6 convert_element_type.200
  1350.5 56.6 %reduce-scatter.23.cloned.1.call-done = f32[256,1024]{1,0:T(8,128)} async-done(((f32[1024,1024]{1,0:T(8,128)}), f32[256,1024]{1,0:T(8,128)}) %reduce-scatter.23.cloned.1.call-update) | async-done | bytes 1048592 | tf_op jit(solution)/shard_map/reduce_scatter | solution.py:94
  1409.0 4.9 all-reduce.1
  1413.9 59.9 %all-reduce = (f32[1,1024]{1,0:T(1,128)}, f32[1,1024]{1,0:T(1,128)}, f32[1,1024]{1,0:T(1,128)}, f32[1,1024]{1,0:T(1,128)}) all-reduce(f32[1,1024]{1,0:T(1,128)S(1)} %bitcast.186, f32[1,1024]{1,0:T(1,128)S(1)} %bitcast.187, f32[1,1024]{1,0:T(1,128)S(1)} %bitcast.184, ...), channel_id=1, replica_groups=mesh['dp'=4,'row'=2,'col'=4] {'dp','col'}, use_global_device_ids=true, to_apply=%region_32.33 | all-reduce | flops 4096 | bytes 32768 | tf_op jit(solution)/shard_map/psum | solution.py:366
  (187 shorter events, 109.6 us)
Async XLA Ops:
  7.2 58.0 %copy-start = (bf16[1,1024,3,512]{3,1,2,0:T(8,128)(2,1)S(1)}, bf16[1,1024,3,512]{3,1,2,0:T(8,128)(2,1)}, u32[]{:S(2)}) copy-start(bf16[1,1024,3,512]{3,1,2,0:T(8,128)(2,1)} %param.18) | copy-start | bytes 9437188
  7.2 58.0 %all-gather.9.cloned.1.call-start = ((), (), s32[]{:S(2)}) async-start(), calls=%async_computation.8 | async-start | bytes 2621440 | tf_op jit(solution)/shard_map/all_gather | solution.py:61
  17.2 130.7 %reduce-scatter.9.cloned.1.call-start = ((), (), s32[]{:S(2)}) async-start(), calls=%async_computation.9 | async-start | bytes 9437184 | tf_op jit(solution)/shard_map/reduce_scatter | solution.py:69
  72.0 133.5 %all-gather.11.cloned.1.call-start = ((), (), s32[]{:S(2)}) async-start(), calls=%async_computation.10 | async-start | bytes 1572864 | tf_op jit(solution)/shard_map/all_gather | solution.py:73
  73.6 85.7 %copy-start.13 = (f32[1024,8]{0,1:T(8,128)}, f32[1024,8]{0,1:T(8,128)S(1)}, u32[]{:S(2)}) copy-start(f32[1024,8]{0,1:T(8,128)S(1)} %get-tuple-element.389) | copy-start | bytes 98308
  164.8 2.4 copy-start.5
  164.8 2.4 copy-start.11
  170.2 0.8 copy-start.12
  175.4 2.4 copy-start.5
  175.4 2.4 copy-start.11
  184.0 103.3 %reduce-scatter.11.cloned.1.call-start = ((), (), s32[]{:S(2)}) async-start(), calls=%async_computation.11 | async-start | bytes 5242880 | tf_op jit(solution)/shard_map/reduce_scatter | solution.py:85
  210.4 84.3 %copy-start.15 = (f32[1,1024]{1,0:T(1,128)S(1)}, f32[1,1024]{1,0:T(1,128)}, u32[]{:S(2)}) copy-start(f32[1,1024]{1,0:T(1,128)} %param.21) | copy-start | bytes 12292
  210.4 84.3 %copy-start.22 = (f32[1,1024]{1,0:T(1,128)S(1)}, f32[1,1024]{1,0:T(1,128)}, u32[]{:S(2)}) copy-start(f32[1,1024]{1,0:T(1,128)} %param.22) | copy-start | bytes 12292
  210.4 124.9 %all-gather.17.cloned.1.call-start = ((), (), s32[]{:S(2)}) async-start(), calls=%async_computation.16 | async-start | bytes 2621440 | tf_op jit(solution)/shard_map/all_gather | solution.py:65
  211.0 170.9 %all-gather.13.cloned.1.call-start = ((), (), s32[]{:S(2)}) async-start(), calls=%async_computation.12 | async-start | bytes 2621440 | tf_op jit(solution)/shard_map/all_gather | solution.py:61
  297.0 157.9 %reduce-scatter.17.cloned.1.call-start = ((), (), s32[]{:S(2)}) async-start(), calls=%async_computation.17 | async-start | bytes 8650752 | tf_op jit(solution)/shard_map/reduce_scatter | solution.py:77
  343.4 247.6 %reduce-scatter.13.cloned.1.call-start = ((), (), s32[]{:S(2)}) async-start(), calls=%async_computation.13 | async-start | bytes 17301504 | tf_op jit(solution)/shard_map/reduce_scatter | solution.py:69
  393.8 279.0 %all-gather.19.cloned.1.call-start = ((), (), s32[]{:S(2)}) async-start(), calls=%async_computation.18 | async-start | bytes 8650752 | tf_op jit(solution)/shard_map/all_gather | solution.py:81
  598.2 118.7 %all-gather.15.cloned.1.call-start = ((), (), s32[]{:S(2)}) async-start(), calls=%async_computation.14 | async-start | bytes 4325376 | tf_op jit(solution)/shard_map/all_gather | solution.py:73
  598.8 197.9 %reduce-scatter.19.cloned.1.call-start = ((), (), s32[]{:S(2)}) async-start(), calls=%async_computation.19 | async-start | bytes 5242880 | tf_op jit(solution)/shard_map/reduce_scatter | solution.py:94
  684.4 192.3 %reduce-scatter.15.cloned.1.call-start = ((), (), s32[]{:S(2)}) async-start(), calls=%async_computation.15 | async-start | bytes 5242880 | tf_op jit(solution)/shard_map/reduce_scatter | solution.py:85
  725.1 202.1 %all-gather.21.cloned.1.call-start = ((), (), s32[]{:S(2)}) async-start(), calls=%async_computation.20 | async-start | bytes 2621440 | tf_op jit(solution)/shard_map/all_gather | solution.py:65
  880.6 81.8 %reduce-scatter.21.cloned.1.call-start = ((), (), s32[]{:S(2)}) async-start(), calls=%async_computation.21 | async-start | bytes 3145728 | tf_op jit(solution)/shard_map/reduce_scatter | solution.py:77
  931.7 162.2 %all-gather.23.cloned.1.call-start = ((), (), s32[]{:S(2)}) async-start(), calls=%async_computation.22 | async-start | bytes 4718592 | tf_op jit(solution)/shard_map/all_gather | solution.py:81
  970.1 2.5 copy-start.7
  972.6 3.5 copy-start.6
  979.2 2.4 copy-start.1
  981.6 1.4 copy-start.2
  981.6 1.4 copy-start.4
  984.0 1.0 copy-start.3
  1000.3 2.5 copy-start.7
  1002.8 4.6 copy-start.6
  1010.5 2.4 copy-start.1
  1012.9 1.4 copy-start.2
  1012.9 1.4 copy-start.4
  1015.3 1.0 copy-start.3
  1048.8 279.2 %all-reduce.8.cloned.1.call-start = ((), (), s32[]{:S(2)}) async-start(), calls=%async_computation.24 | async-start | bytes 25690112 | tf_op jit(solution)/shard_map/psum | solution.py:363
  1049.1 7.4 copy-start.24
  1056.4 11.2 copy-start.10
  1056.4 11.2 copy-start.25
  1101.6 305.5 %reduce-scatter.23.cloned.1.call-start = ((), (), s32[]{:S(2)}) async-start(), calls=%async_computation.23 | async-start | bytes 5242880 | tf_op jit(solution)/shard_map/reduce_scatter | solution.py:94
  1330.8 12.8 copy-start.9
  1343.6 3.3 copy-start.8
  1346.8 60.3 %copy-start.14 = (f32[1,1024]{1,0:T(1,128)S(1)}, f32[1,1024]{1,0:T(1,128)}, u32[]{:S(2)}) copy-start(f32[1,1024]{1,0:T(1,128)} %param.16) | copy-start | bytes 12292
  1346.8 60.3 %copy-start.19 = (f32[256]{0:T(256)S(1)}, f32[256]{0:T(256)}, u32[]{:S(2)}) copy-start(f32[256]{0:T(256)} %copy-done.18) | copy-start | bytes 3076
  1346.8 60.3 %copy-start.21 = (f32[256]{0:T(256)S(1)}, f32[256]{0:T(256)}, u32[]{:S(2)}) copy-start(f32[256]{0:T(256)} %copy-done.20) | copy-start | bytes 3076
  1346.8 67.1 %copy-start.16 = (f32[1024]{0:T(1024)S(1)}, f32[1024]{0:T(1024)}, u32[]{:S(2)}) copy-start(f32[1024]{0:T(1024)} %get-tuple-element.300) | copy-start | bytes 12292
  1346.8 67.1 %copy-start.17 = (f32[1024]{0:T(1024)S(1)}, f32[1024]{0:T(1024)}, u32[]{:S(2)}) copy-start(f32[1024]{0:T(1024)} %get-tuple-element.306) | copy-start | bytes 12292
  (4 other events, 2.6 us)
Sparse Core Ops, SparseCore 0:
  17.4 47.7 all-gather.8
  72.2 75.7 reduce-scatter.8
  184.2 21.3 all-gather.10
  210.5 76.7 reduce-scatter.10
  288.7 46.4 all-gather.16
  337.2 44.6 all-gather.12
  384.8 70.0 reduce-scatter.16
  457.9 133.1 reduce-scatter.12
  598.3 74.4 all-gather.18
  674.9 41.9 all-gather.14
  719.9 76.7 reduce-scatter.18
  799.4 77.2 reduce-scatter.14
  880.7 46.4 all-gather.20
  931.8 30.5 reduce-scatter.20
  1048.9 44.9 all-gather.22
  1101.7 226.2 all-reduce.7
  1330.1 76.9 reduce-scatter.22
where the time goes:
time: 1490 us; the launch traced here: 1480 us
  waiting for transfers between devices  1100 us (74%)
  matrix products  127 us (9%)
  blocking collectives  88.4 us (6%)
  other arithmetic  67.5 us (5%)
  local copies, waits for them, and re-layouts  66.9 us (4%)
    reduce_scatter x2, waiting for transfers between devices, split_units(): return lax.psum_scatter(partial_sum, 'row', scatter_dimension=2, tiled=True)  211 us
    psum x1, waiting for transfers between devices, local(): lax.psum(stack_gate.astype(jnp.bfloat16), 'dp').astype(jnp.float32)  209 us
    reduce_scatter x2, waiting for transfers between devices, branch_sum(): lax.psum_scatter(jnp.dot(full_rows, weight_block, preferred_element_type=...  149 us
    reduce_scatter x2, waiting for transfers between devices, input_sum(): lax.psum_scatter(jnp.einsum('stk,dtk->sd', grad_full, weight_block, prefe...  128 us
    all_gather x2, waiting for transfers between devices, join_unit_grads(): return lax.all_gather(local_units, 'row', axis=2, tiled=True)  98 us
    all_gather x2, waiting for transfers between devices, gather_tokens(): return lax.all_gather(local_low, 'col', axis=0, tiled=True)  86.3 us
    all_gather x2, waiting for transfers between devices, gather_gradient(): return lax.all_gather(local_low, 'col', axis=0, tiled=True)  84.5 us
    reduce_scatter x2, waiting for transfers between devices, split_unit_grads(): return lax.psum_scatter(partial_sum, 'row', scatter_dimension=1, tiled=True)  83 us
  transfers between devices with their start and end apart: 17, of which 17 were waited for; matrix products, arithmetic and copies ran while one was open for 7% of the time, Pallas kernels for 0%

commit v1 on v0

--- a/solution.py
+++ b/solution.py
@@ -1,3 +1,4 @@
+import functools
 import math
 import jax
 import jax.numpy as jnp
@@ -8,6 +9,28 @@
 ROT = 16
 LENGTH = 1024
 EPSILON = 1e-05
+
+
+def sites_fill(mine_x, dim_no):
+    world_n = lax.axis_size("col")
+    sheets = []
+    for dd in [*range(world_n)]:
+        sheets.append((dd, (dd + 1) % world_n))
+    history = []
+    for dd in tuple(range(world_n)):
+        history.append((dd, (dd - 1) % world_n))
+    g_now, finding = ([mine_x], [mine_x])
+    for _ in range(world_n // 2):
+        g_now.append(lax.ppermute(g_now[-1], axis_name="col", perm=sheets))
+    for _ in tuple(range((world_n - 1) // 2)):
+        finding.append(lax.ppermute(finding[-1], axis_name="col", perm=history))
+    value_now = jnp.concatenate([*g_now[::-1], *finding[1:]], axis=dim_no)
+    return jnp.roll(
+        value_now, (lax.axis_index("col") - world_n // 2) * mine_x.shape[dim_no], axis=dim_no
+    )
+
+
+state_marks_for = functools.partial(sites_fill, dim_no=0)
 
 
 def rotary_tables(tokens):
@@ -58,7 +81,7 @@
 
 
 def gather_tokens(local_low):
-    return lax.all_gather(local_low, "col", axis=0, tiled=True)
+    return state_marks_for(local_low)
 
 
 def gather_gradient(local_low):

time: 1490 us -> 1450 us (0.973)
  waiting for transfers between devices: 1100 us -> 1030 us
    all_gather x2, waiting for transfers between devices: 86.3 us -> 0.01 us  [weight_product(): lax.all_gather(local_low, 'col', axis=0, tiled=True)]
    ppermute x0 -> x6, waiting for transfers between devices: none -> 52.5 us  [the longest x4 46.2 us: sites_fill(): g_now.append(lax.ppermute(g_now[-1], axis_name='col', perm=sheets))]
    reduce_scatter x2, waiting for transfers between devices: 83 us -> 41 us  [split_unit_grads(): return lax.psum_scatter(partial_sum, 'row', scatter_dimension=1, tiled=True)]
    ppermute x0 -> x6, starting transfers between devices: none -> 22.3 us  [the longest x4 17.9 us: sites_fill(): g_now.append(lax.ppermute(g_now[-1], axis_name='col', perm=sheets))]
  transfers between devices with their start and end apart: 17 -> 23, of which waited for: 17 -> 21; matrix products, arithmetic and copies ran while one was open for 7% -> 13% of each run, Pallas kernels for 0% -> 0%
where the time goes in v1:
time: 1450 us; the launch traced here: 1440 us
  waiting for transfers between devices  1030 us (71%)
  matrix products  134 us (9%)
  blocking collectives  88.4 us (6%)
  other arithmetic  67.5 us (5%)
  local copies, waits for them, and re-layouts  66.9 us (5%)
  starting transfers between devices  24 us (2%)
  between operations  14.6 us (1%)
    reduce_scatter x2, waiting for transfers between devices, split_units(): return lax.psum_scatter(partial_sum, 'row', scatter_dimension=2, tiled=True)  211 us
    psum x1, waiting for transfers between devices, local(): lax.psum(stack_gate.astype(jnp.bfloat16), 'dp').astype(jnp.float32)  209 us
    reduce_scatter x2, waiting for transfers between devices, branch_sum(): lax.psum_scatter(jnp.dot(full_rows, weight_block, preferred_element_type=...  142 us
    reduce_scatter x2, waiting for transfers between devices, input_sum(): lax.psum_scatter(jnp.einsum('stk,dtk->sd', grad_full, weight_block, prefe...  128 us
    all_gather x2, waiting for transfers between devices, join_unit_grads(): return lax.all_gather(local_units, 'row', axis=2, tiled=True)  105 us
    all_gather x2, waiting for transfers between devices, gather_gradient(): return lax.all_gather(local_low, 'col', axis=0, tiled=True)  89.3 us
    psum x1, blocking collectives, local(): lax.psum((jnp.stack(gain_a_grads), jnp.stack(shift_a_grads), jnp.stack(ga...  59.9 us
    all_gather x2, waiting for transfers between devices, join_units(): return lax.all_gather(local_units, 'row', axis=1, tiled=True)  53.1 us
  transfers between devices with their start and end apart: 23, of which 21 were waited for; matrix products, arithmetic and copies ran while one was open for 13% of the time, Pallas kernels for 0%

profile of v1, /device:TPU:0, one launch (start us, length us, event | category | flops | bytes accessed | tf_op | source)
XLA Modules:
  0.0 1436.4 jit_solution(10117988568369983005)
XLA Ops:
  8.7 5.8 all-reduce.4
  21.4 13.2 collective-permute-done
  34.6 6.7 collective-permute-start.1
  44.6 10.4 collective-permute-done.1
  55.0 9.9 fusion.42
  66.4 75.1 %reduce-scatter.9.cloned.1.call-done = f32[1024,3,256]{2,0,1:T(8,128)} async-done(((f32[1024,3,512]{2,0,1:T(8,128)}), f32[1024,3,256]{2,0,1:T(8,128)}) %reduce-scatter.9.cloned.1.call-update) | async-done | bytes 3145744 | tf_op jit(solution)/shard_map/reduce_scatter | solution.py:92
  141.5 3.8 broadcast_add_fusion
  153.9 21.1 %while.31 = (s32[]{:T(128)}, bf16[2,512,4,64]{1,3,2,0:T(8,128)(2,1)}, f32[2,4,512]{2,1,0:T(4,128)S(1)}, s32[2]{0:T(128)S(1)}, bf16[1024,4,64]{0,2,1:T(8,128)(2,1...) while((s32[]{:T(128)}, ...), condition=%wide.region_8.10_spmd, body=%wide.region_5.9_spmd.sunk | while | flops 562559488 | bytes 35459536 | solution.py:167
  178.5 20.5 %all-gather.9.cloned.1.call-done = bf16[1024,512]{0,1:T(8,128)(2,1)} async-done(((bf16[1024,256]{0,1:T(8,128)(2,1)}), bf16[1024,512]{0,1:T(8,128)(2,1)}) %all-gather.9.cloned.1.call-update) | async-done | bytes 1048592 | tf_op jit(solution)/shard_map/all_gather | solution.py:96
  199.0 4.8 fusion.95
  203.9 42.7 %all-gather.13.cloned.1.call-done = bf16[1024,1024]{1,0:T(8,128)(2,1)} async-done(((bf16[256,1024]{1,0:T(8,128)(2,1)}), bf16[1024,1024]{1,0:T(8,128)(2,1)}) %all-gather.13.cloned.1.call-update) | async-done | bytes 2097168 | tf_op jit(solution)/shard_map/all_gather | solution.py:88
  246.6 8.3 fusion.44
  255.0 69.9 %reduce-scatter.11.cloned.1.call-done = f32[256,1024]{1,0:T(8,128)} async-done(((f32[1024,1024]{1,0:T(8,128)}), f32[256,1024]{1,0:T(8,128)}) %reduce-scatter.11.cloned.1.call-update) | async-done | bytes 1048592 | tf_op jit(solution)/shard_map/reduce_scatter | solution.py:108
  327.4 4.9 all-reduce.3
  338.4 13.1 collective-permute-done.3
  351.5 7.6 collective-permute-start.4
  362.1 9.6 collective-permute-done.4
  371.7 15.9 %fusion.35 = f32[1024,2,1408]{0,2,1:T(8,128)} fusion(bf16[1024,2,1408]{2,1,0:T(2,128)(2,1)} %bitcast.191, s32[]{:T(128)S(6)} %select_n.107, bf16[256,1024]{1,0:T(8,128)(2,1)S(1)} %collective-permute-done.4, bf16[256,1024]{1,0:T(8,128)(2,1)S(1)} %collective-permute-done.3, bf16[256,1024]{1,0:T(8,128)(2,1)} %add_convert_fusion.1, ...), kind=kOutput, calls=%fused_computation.45 | convolution fusion | flops 5922357248 | bytes 19398660 | tf_op jit(solution)/shard_map/sd,dtf->stf/dot_general | solution.py:256
  387.7 11.9 reduce-scatter.17.cloned.1.call-done
  399.5 136.0 %reduce-scatter.13.cloned.1.call-done = f32[1024,2,704]{0,2,1:T(8,128)} async-done(((f32[1024,2,1408]{0,2,1:T(8,128)}), f32[1024,2,704]{0,2,1:T(8,128)}) %reduce-scatter.13.cloned.1.call-update) | async-done | bytes 5767184 | tf_op jit(solution)/shard_map/reduce_scatter | solution.py:92
  535.6 5.3 fusion.77
  543.9 73.4 %all-gather.15.cloned.1.call-done = bf16[1024,2,1408]{0,2,1:T(8,128)(2,1)} async-done(((bf16[1024,2,704]{0,2,1:T(8,128)(2,1)}), bf16[1024,2,1408]{0,2,1:T(8,128)(2,1)}) %all-gather.15.cloned.1.call-update) | async-done | bytes 5767184 | tf_op jit(solution)/shard_map/all_gather | solution.py:104
  617.4 11.5 fusion.51
  628.9 32.7 %all-gather.11.cloned.1.call-done = bf16[1024,1408]{0,1:T(8,128)(2,1)} async-done(((bf16[1024,704]{0,1:T(8,128)(2,1)}), bf16[1024,1408]{0,1:T(8,128)(2,1)}) %all-gather.11.cloned.1.call-update) | async-done | bytes 2883600 | tf_op jit(solution)/shard_map/all_gather | solution.py:96
  661.6 8.2 fusion.46
  669.8 71.5 %reduce-scatter.19.cloned.1.call-done = f32[256,1024]{1,0:T(8,128)} async-done(((f32[1024,1024]{1,0:T(8,128)}), f32[256,1024]{1,0:T(8,128)}) %reduce-scatter.19.cloned.1.call-update) | async-done | bytes 1048592 | tf_op jit(solution)/shard_map/reduce_scatter | solution.py:117
  744.0 4.9 all-reduce.2
  748.9 72.5 %reduce-scatter.15.cloned.1.call-done = f32[256,1024]{1,0:T(8,128)} async-done(((f32[1024,1024]{1,0:T(8,128)}), f32[256,1024]{1,0:T(8,128)}) %reduce-scatter.15.cloned.1.call-update) | async-done | bytes 1048592 | tf_op jit(solution)/shard_map/reduce_scatter | solution.py:108
  821.4 3.8 fusion.109
  825.3 46.5 %all-gather.17.cloned.1.call-done = bf16[1024,1024]{1,0:T(8,128)(2,1)} async-done(((bf16[256,1024]{1,0:T(8,128)(2,1)}), bf16[1024,1024]{1,0:T(8,128)(2,1)}) %all-gather.17.cloned.1.call-update) | async-done | bytes 2097168 | tf_op jit(solution)/shard_map/all_gather | solution.py:88
  871.9 4.5 fusion.93
  877.9 29.1 %reduce-scatter.21.cloned.1.call-done = f32[1024,256]{1,0:T(8,128)} async-done(((f32[1024,512]{1,0:T(8,128)}), f32[1024,256]{1,0:T(8,128)}) %reduce-scatter.21.cloned.1.call-update) | async-done | bytes 1048592 | tf_op jit(solution)/shard_map/reduce_scatter | solution.py:100
  911.1 61.6 %while.32 = (s32[]{:T(128)}, f32[1024,4,64]{0,2,1:T(8,128)}, f32[1024,4,64]{0,2,1:T(8,128)}, f32[2,512,4,64]{1,0,3,2:T(2,128)}, s32[2]{0:T(128)S(1)}, /*index=5*...) while((s32[]{:T(128)}, f32[1024,4,64]{0,2,1:T(8,128)}, ...), condition=%wide.region_25.27_spmd.clone, body=%wide.region_23.26_spmd.clone.sunk | while | flops 1375599104 | bytes 91288184 | solution.py:206
  931.0 10.4 dynamic_update_slice.28
  947.5 4.5 fusion.163
  962.4 10.4 dynamic_update_slice.28
  993.8 7.2 fusion.39
  1001.0 11.1 convert_bitcast_fusion
  1014.4 31.9 %all-gather.19.cloned.1.call-done = bf16[1024,3,512]{2,0,1:T(8,128)(2,1)} async-done(((bf16[1024,3,256]{2,0,1:T(8,128)(2,1)}), bf16[1024,3,512]{2,0,1:T(8,128)(2,1)}) %all-gather.19.cloned.1.call-update) | async-done | bytes 3145744 | tf_op jit(solution)/shard_map/all_gather | solution.py:104
  1046.3 7.7 convert_bitcast_fusion.1
  1054.1 6.9 fusion.48
  1063.4 7.9 psum.130
  1071.9 208.6 %all-reduce.8.cloned.1.call-done = (bf16[1,1024,2,1408]{3,1,2,0:T(8,128)(2,1)}, bf16[1,1024,3,512]{3,1,2,0:T(8,128)(2,1)}, bf16[1,512,1024]{2,1,0:T(8,128)(2,1)}, bf16[1,1408,1024]{2,1,0:T(8,128)(2,1)}) async-done(((bf16[1,1024,2,1408]{3,1,2,0:T(8,128)(2,1)}, bf16[1,1024,3,512]{3,1,2,0:T(8,128)(2,1)}, bf16[1,512,1024]{2,1,0:T(8,128)(2,1)}, bf16[1,1408,1024]{2,1,0:T(8,128)(2,1)}), ...) | async-done | bytes 12845072 | tf_op jit(solution)/shard_map/psum | solution.py:386
  1283.2 12.8 copy.45
  1299.3 3.6 convert_element_type.200
  1302.9 56.6 %reduce-scatter.23.cloned.1.call-done = f32[256,1024]{1,0:T(8,128)} async-done(((f32[1024,1024]{1,0:T(8,128)}), f32[256,1024]{1,0:T(8,128)}) %reduce-scatter.23.cloned.1.call-update) | async-done | bytes 1048592 | tf_op jit(solution)/shard_map/reduce_scatter | solution.py:117
  1361.4 4.9 all-reduce.1
  1366.4 59.9 %all-reduce = (f32[1,1024]{1,0:T(1,128)}, f32[1,1024]{1,0:T(1,128)}, f32[1,1024]{1,0:T(1,128)}, f32[1,1024]{1,0:T(1,128)}) all-reduce(f32[1,1024]{1,0:T(1,128)S(1)} %bitcast.186, f32[1,1024]{1,0:T(1,128)S(1)} %bitcast.187, f32[1,1024]{1,0:T(1,128)S(1)} %bitcast.184, ...), channel_id=1, replica_groups=mesh['dp'=4,'row'=2,'col'=4] {'dp','col'}, use_global_device_ids=true, to_apply=%region_32.34 | all-reduce | flops 4096 | bytes 32768 | tf_op jit(solution)/shard_map/psum | solution.py:389
  (197 shorter events, 136.2 us)
Async XLA Ops:
  7.2 47.8 %copy-start = (bf16[1,1024,3,512]{3,1,2,0:T(8,128)(2,1)S(1)}, bf16[1,1024,3,512]{3,1,2,0:T(8,128)(2,1)}, u32[]{:S(2)}) copy-start(bf16[1,1024,3,512]{3,1,2,0:T(8,128)(2,1)} %param.20) | copy-start | bytes 9437188
  7.2 134.3 %reduce-scatter.9.cloned.1.call-start = ((), (), s32[]{:S(2)}) async-start(), calls=%async_computation.8 | async-start | bytes 9437184 | tf_op jit(solution)/shard_map/reduce_scatter | solution.py:92
  17.2 17.3 %collective-permute-start = (bf16[256,1024]{1,0:T(8,128)(2,1)}, bf16[256,1024]{1,0:T(8,128)(2,1)}, u32[]{:S(2)}, u32[]{:S(2)}) collective-permute-start(bf16[256,1024]{1,0:T(8,128)(2,1)} %fusion.85), channel_id=1, source_target_pairs={{0,1},{1,2},{2,3},{3,0},{4,5},{5,6},{6,7},{7,4},{8,9},{9,10},{10,1... | collective-permute-start | bytes 1572872 | tf_op jit(solution)/shard_map/ppermute | solution.py:24
  19.3 25.2 %collective-permute-start.2 = (bf16[256,1024]{1,0:T(8,128)(2,1)}, bf16[256,1024]{1,0:T(8,128)(2,1)}, u32[]{:S(2)}, u32[]{:S(2)}) collective-permute-start(bf16[256,1024]{1,0:T(8,128)(2,1)} %fusion.85), channel_id=1, source_target_pairs={{0,3},{1,0},{2,1},{3,2},{4,7},{5,4},{6,5},{7,6},{8,11},{9,8},{10,9... | collective-permute-start | bytes 1572872 | tf_op jit(solution)/shard_map/ppermute | solution.py:26
  34.6 20.4 %collective-permute-start.1 = (bf16[256,1024]{1,0:T(8,128)(2,1)}, bf16[256,1024]{1,0:T(8,128)(2,1)}, u32[]{:S(2)}, u32[]{:S(2)}) collective-permute-start(bf16[256,1024]{1,0:T(8,128)(2,1)} %collective-permute-done), channel_id=1, source_target_pairs={{0,1},{1,2},{2,3},{3,0},{4,5},{5,6},{6,7},{7,4},{8,9},{9,10},{10,1... | collective-permute-start | bytes 1572872 | tf_op jit(solution)/shard_map/ppermute | solution.py:24
  64.9 134.1 %all-gather.9.cloned.1.call-start = ((), (), s32[]{:S(2)}) async-start(), calls=%async_computation.9 | async-start | bytes 1572864 | tf_op jit(solution)/shard_map/all_gather | solution.py:96
  66.4 86.3 %copy-start.13 = (f32[1024,8]{0,1:T(8,128)}, f32[1024,8]{0,1:T(8,128)S(1)}, u32[]{:S(2)}) copy-start(f32[1024,8]{0,1:T(8,128)S(1)} %get-tuple-element.390) | copy-start | bytes 98308
  158.3 2.4 copy-start.5
  158.3 2.4 copy-start.11
  168.9 2.4 copy-start.5
  168.9 2.4 copy-start.11
  177.5 69.1 %all-gather.13.cloned.1.call-start = ((), (), s32[]{:S(2)}) async-start(), calls=%async_computation.14 | async-start | bytes 2621440 | tf_op jit(solution)/shard_map/all_gather | solution.py:88
  178.2 146.7 %reduce-scatter.11.cloned.1.call-start = ((), (), s32[]{:S(2)}) async-start(), calls=%async_computation.10 | async-start | bytes 5242880 | tf_op jit(solution)/shard_map/reduce_scatter | solution.py:108
  203.8 195.7 %reduce-scatter.17.cloned.1.call-start = ((), (), s32[]{:S(2)}) async-start(), calls=%async_computation.15 | async-start | bytes 8650752 | tf_op jit(solution)/shard_map/reduce_scatter | solution.py:100
  254.9 77.4 %copy-start.15 = (f32[1,1024]{1,0:T(1,128)S(1)}, f32[1,1024]{1,0:T(1,128)}, u32[]{:S(2)}) copy-start(f32[1,1024]{1,0:T(1,128)} %param.23) | copy-start | bytes 12292
  254.9 77.4 %copy-start.22 = (f32[1,1024]{1,0:T(1,128)S(1)}, f32[1,1024]{1,0:T(1,128)}, u32[]{:S(2)}) copy-start(f32[1,1024]{1,0:T(1,128)} %param.24) | copy-start | bytes 12292
  255.0 280.6 %reduce-scatter.13.cloned.1.call-start = ((), (), s32[]{:S(2)}) async-start(), calls=%async_computation.11 | async-start | bytes 17301504 | tf_op jit(solution)/shard_map/reduce_scatter | solution.py:92
  334.6 16.9 %collective-permute-start.3 = (bf16[256,1024]{1,0:T(8,128)(2,1)}, bf16[256,1024]{1,0:T(8,128)(2,1)S(1)}, u32[]{:S(2)}, u32[]{:S(2)}) collective-permute-start(bf16[256,1024]{1,0:T(8,128)(2,1)} %add_convert_fusion.1), channel_id=1, source_target_pairs={{0,1},{1,2},{2,3},{3,0},{4,5},{5,6},{6,7},{7,4},{8,9},{9,10},{10,1... | collective-permute-start | bytes 1572872 | tf_op jit(solution)/shard_map/ppermute | solution.py:24
  336.1 26.0 %collective-permute-start.5 = (bf16[256,1024]{1,0:T(8,128)(2,1)}, bf16[256,1024]{1,0:T(8,128)(2,1)S(1)}, u32[]{:S(2)}, u32[]{:S(2)}) collective-permute-start(bf16[256,1024]{1,0:T(8,128)(2,1)} %add_convert_fusion.1), channel_id=1, source_target_pairs={{0,3},{1,0},{2,1},{3,2},{4,7},{5,4},{6,5},{7,6},{8,11},{9,8},{10,9... | collective-permute-start | bytes 1572872 | tf_op jit(solution)/shard_map/ppermute | solution.py:26
  351.5 20.2 %collective-permute-start.4 = (bf16[256,1024]{1,0:T(8,128)(2,1)S(1)}, bf16[256,1024]{1,0:T(8,128)(2,1)S(1)}, u32[]{:S(2)}, u32[]{:S(2)}) collective-permute-start(bf16[256,1024]{1,0:T(8,128)(2,1)S(1)} %collective-permute-done.3), channel_id=1, source_target_pairs={{0,1},{1,2},{2,3},{3,0},{4,5},{5,6},{6,7},{7,4},{8,9},{9,10},{10,1... | collective-permute-start | bytes 1572872 | tf_op jit(solution)/shard_map/ppermute | solution.py:24
  387.6 229.7 %all-gather.15.cloned.1.call-start = ((), (), s32[]{:S(2)}) async-start(), calls=%async_computation.16 | async-start | bytes 8650752 | tf_op jit(solution)/shard_map/all_gather | solution.py:104
  542.7 118.9 %all-gather.11.cloned.1.call-start = ((), (), s32[]{:S(2)}) async-start(), calls=%async_computation.12 | async-start | bytes 4325376 | tf_op jit(solution)/shard_map/all_gather | solution.py:96
  543.5 197.9 %reduce-scatter.19.cloned.1.call-start = ((), (), s32[]{:S(2)}) async-start(), calls=%async_computation.17 | async-start | bytes 5242880 | tf_op jit(solution)/shard_map/reduce_scatter | solution.py:117
  628.9 192.5 %reduce-scatter.15.cloned.1.call-start = ((), (), s32[]{:S(2)}) async-start(), calls=%async_computation.13 | async-start | bytes 5242880 | tf_op jit(solution)/shard_map/reduce_scatter | solution.py:108
  669.8 202.1 %all-gather.17.cloned.1.call-start = ((), (), s32[]{:S(2)}) async-start(), calls=%async_computation.18 | async-start | bytes 2621440 | tf_op jit(solution)/shard_map/all_gather | solution.py:88
  825.3 81.8 %reduce-scatter.21.cloned.1.call-start = ((), (), s32[]{:S(2)}) async-start(), calls=%async_computation.19 | async-start | bytes 3145728 | tf_op jit(solution)/shard_map/reduce_scatter | solution.py:100
  876.4 124.7 %all-gather.23.cloned.1.call-start = ((), (), s32[]{:S(2)}) async-start(), calls=%async_computation.23 | async-start | bytes 2621440 | tf_op jit(solution)/shard_map/all_gather | solution.py:129
  877.1 137.3 %all-gather.21.cloned.1.call-start = ((), (), s32[]{:S(2)}) async-start(), calls=%async_computation.22 | async-start | bytes 2621440 | tf_op jit(solution)/shard_map/all_gather | solution.py:129
  877.7 168.6 %all-gather.19.cloned.1.call-start = ((), (), s32[]{:S(2)}) async-start(), calls=%async_computation.20 | async-start | bytes 4718592 | tf_op jit(solution)/shard_map/all_gather | solution.py:104
  914.7 2.5 copy-start.7
  917.3 3.5 copy-start.6
  923.9 2.4 copy-start.1
  926.3 1.4 copy-start.2
  945.0 2.5 copy-start.7
  947.5 4.6 copy-start.6
  955.2 2.4 copy-start.1
  957.6 1.4 copy-start.2
  993.6 286.9 %all-reduce.8.cloned.1.call-start = ((), (), s32[]{:S(2)}) async-start(), calls=%async_computation.24 | async-start | bytes 25690112 | tf_op jit(solution)/shard_map/psum | solution.py:386
  1001.0 11.1 copy-start.10
  1001.0 11.1 copy-start.24
  1054.0 305.5 %reduce-scatter.23.cloned.1.call-start = ((), (), s32[]{:S(2)}) async-start(), calls=%async_computation.21 | async-start | bytes 5242880 | tf_op jit(solution)/shard_map/reduce_scatter | solution.py:117
  1283.2 12.8 copy-start.9
  1296.0 3.3 copy-start.8
  1299.3 60.3 %copy-start.14 = (f32[1,1024]{1,0:T(1,128)S(1)}, f32[1,1024]{1,0:T(1,128)}, u32[]{:S(2)}) copy-start(f32[1,1024]{1,0:T(1,128)} %param.18) | copy-start | bytes 12292
  1299.3 60.3 %copy-start.19 = (f32[256]{0:T(256)S(1)}, f32[256]{0:T(256)}, u32[]{:S(2)}) copy-start(f32[256]{0:T(256)} %copy-done.18) | copy-start | bytes 3076
  1299.3 60.3 %copy-start.21 = (f32[256]{0:T(256)S(1)}, f32[256]{0:T(256)}, u32[]{:S(2)}) copy-start(f32[256]{0:T(256)} %copy-done.20) | copy-start | bytes 3076
  1299.3 67.1 %copy-start.16 = (f32[1024]{0:T(1024)S(1)}, f32[1024]{0:T(1024)}, u32[]{:S(2)}) copy-start(f32[1024]{0:T(1024)} %get-tuple-element.301) | copy-start | bytes 12292
  1299.3 67.1 %copy-start.17 = (f32[1024]{0:T(1024)S(1)}, f32[1024]{0:T(1024)}, u32[]{:S(2)}) copy-start(f32[1024]{0:T(1024)} %get-tuple-element.307) | copy-start | bytes 12292
  (9 other events, 8.2 us)
Sparse Core Ops, SparseCore 0:
  65.0 76.3 reduce-scatter.8
  177.6 21.2 all-gather.8
  200.6 45.9 all-gather.12
  249.4 75.4 reduce-scatter.10
  327.7 71.8 reduce-scatter.16
  402.4 133.1 reduce-scatter.12
  542.9 74.4 all-gather.14
  619.6 41.9 all-gather.10
  664.6 76.7 reduce-scatter.18
  744.1 77.2 reduce-scatter.14
  825.4 46.4 all-gather.16
  876.5 30.5 reduce-scatter.20
  908.6 45.9 all-gather.22
  956.0 44.6 all-gather.20
  1002.7 43.6 all-gather.18
  1054.1 226.2 all-reduce.7
  1282.6 76.9 reduce-scatter.22
